TPU v7x, 512 devices: a whole 4x8x8 slice. The times are simulated.
512 devices in a mesh: row: 16 (over x, y_lo), col: 32 (over y_hi, z, core).
Axes of the slice: x: 4, y: 8 (y_hi: 2, y_lo: 4; y = y_hi * 4 + y_lo), z: 8, core: 2. Of those that a mesh axis runs over, the one named last changes fastest.
Arguments:
- bricks: bfloat16 [16, 32, 2, 16, 128, 128], P('row', 'col'), may hold values from -393216 to 393216
- brick_coords: int32 [16, 32, 3, 2], P('row', 'col'), may hold values from 0 to 31, as said below
- brick_counts: int32 [16, 32], P('row', 'col'), may hold values from 0 to 2, as said below
- step_sizes: float32 [2, 3], replicated, may hold values from 0.3 to 1
- init_a: float32 [16, 512, 256], P('row', 'col'), may hold values from -6 to 6
- init_b: float32 [32, 256, 256], P('col', 'row'), may hold values from -6 to 6
- init_c: float32 [512, 256], replicated, may hold values from -6 to 6
Outputs:
- factor_a: float32 [16, 512, 256], P('row', 'col')
- factor_b: float32 [32, 256, 256], P('col', 'row')
- factor_c: float32 [512, 256], replicated
Inputs may be any that keep to these rules, and one draw needn't show every extreme that they name: brick_counts of rows r and (r + half of the row axis) mod the row axis in one column add up to at most 3; some device holds 2 bricks. `brick_coords`: component 0 is below 4, component 1 below 2, component 2 below 32; dead slots hold arbitrary positions.
All inputs are finite; a program needn't handle non-finite values.
Results may differ from a plain program's by a relative error of at most 0.0003.
The roundings to bfloat16 on the way count: a program that leaves them out, or rounds other values in their place, can miss the bound.
Values may be sent and summed in bfloat16 or wider, within the bound.
No kernel may reach another device: no remote copies, remote signals or barrier semaphores. Data moves between devices by JAX's collectives and lax.ppermute only.
A program may use at most 64 MiB of HBM per device.

v0:
```python
import jax
import jax.numpy as jnp
from jax import lax
from jax.sharding import PartitionSpec as P


def brick_terms(brick, a_tile, b_tile, c_rows):
    depth, tile, _ = brick.shape
    wide = jnp.dot(
        brick.reshape(depth * tile, tile), b_tile, preferred_element_type=jnp.float32
    ).reshape(depth, tile, -1)
    c_wide = c_rows.astype(jnp.float32)[:, None, :]
    along_a = jnp.sum(wide * c_wide, axis=0)
    deep = jnp.einsum("kij,ir->kjr", brick, a_tile, preferred_element_type=jnp.float32)
    along_b = jnp.sum(deep * c_wide, axis=0)
    along_c = jnp.sum(deep * b_tile.astype(jnp.float32)[None, :, :], axis=1)
    return (along_a, along_b, along_c)


def add_tile(total, delta, start):
    old = lax.dynamic_slice_in_dim(total, start, delta.shape[0], 0)
    return lax.dynamic_update_slice_in_dim(total, old + delta, start, 0)


def gram(values):
    return jnp.dot(values.T, values, preferred_element_type=jnp.float32)


def project(state, hess, drive, rate):
    scale = jnp.sum(jnp.abs(hess), axis=1) + 1e-06
    slope = (
        jnp.dot(state, hess, precision=lax.Precision.HIGHEST, preferred_element_type=jnp.float32)
        - drive
    )
    return jnp.maximum(state - rate * slope / scale[None, :], 0.0)


def shards(bricks, brick_coords, brick_counts, step_sizes, init_a, init_b, init_c):
    slab = bricks[0, 0]
    places = brick_coords[0, 0]
    own = brick_counts[0, 0]
    depth = slab.shape[1]
    tile = slab.shape[2]
    sweeps = step_sizes.shape[0]
    state_a = init_a[0]
    state_b = init_b[0]
    state_c = init_c
    for sweep in range(sweeps):
        a_bf = state_a.astype(jnp.bfloat16)
        b_bf = state_b.astype(jnp.bfloat16)
        c_bf = state_c.astype(jnp.bfloat16)
        a_range = lax.all_gather(a_bf, "col", axis=0, tiled=True)
        b_range = lax.all_gather(b_bf, "row", axis=0, tiled=True)
        local_ga = gram(a_bf)
        local_gb = gram(b_bf)
        gram_a, gram_b = lax.psum((local_ga, local_gb), ("row", "col"))
        gram_c = gram(c_bf)

        def own_step(slot, carry):
            total_a, total_b, total_c = carry
            brick = lax.dynamic_index_in_dim(slab, slot, 0, keepdims=False)
            spot = lax.dynamic_index_in_dim(places, slot, 1, keepdims=False)
            i_low = spot[0] * tile
            j_low = spot[1] * tile
            k_low = spot[2] * depth
            a_tile = lax.dynamic_slice_in_dim(a_range, i_low, tile, 0)
            b_tile = lax.dynamic_slice_in_dim(b_range, j_low, tile, 0)
            c_rows = lax.dynamic_slice_in_dim(c_bf, k_low, depth, 0)
            delta_a, delta_b, delta_c = brick_terms(brick, a_tile, b_tile, c_rows)
            return (
                add_tile(total_a, delta_a, i_low),
                add_tile(total_b, delta_b, j_low),
                add_tile(total_c, delta_c, k_low),
            )

        empty = (
            jnp.zeros(a_range.shape, jnp.float32),
            jnp.zeros(b_range.shape, jnp.float32),
            jnp.zeros(c_bf.shape, jnp.float32),
        )
        drive_a, drive_b, drive_c = lax.fori_loop(0, own, own_step, empty)
        mine_a = lax.psum_scatter(drive_a, "col", scatter_dimension=0, tiled=True)
        mine_b = lax.psum_scatter(drive_b, "row", scatter_dimension=0, tiled=True)
        summed_c = lax.psum(drive_c, ("row", "col"))
        new_c = project(state_c, gram_a * gram_b, summed_c, step_sizes[sweep, 2])
        new_a = project(state_a, gram_b * gram_c, mine_a, step_sizes[sweep, 0])
        new_b = project(state_b, gram_a * gram_c, mine_b, step_sizes[sweep, 1])
        state_a, state_b, state_c = (new_a, new_b, new_c)
    return (state_a[None], state_b[None], state_c)


def solution(mesh):
    placed = (
        P("row", "col", None, None, None, None),
        P("row", "col", None, None),
        P("row", "col"),
        P(),
        P("row", "col", None),
        P("col", "row", None),
        P(),
    )
    return jax.shard_map(
        shards,
        mesh=mesh,
        in_specs=placed,
        out_specs=(P("row", "col", None), P("col", "row", None), P()),
        check_vma=False,
    )
```

profile of v0, /device:TPU:17, one launch (start us, length us, event | category | flops | bytes accessed | tf_op | source)
XLA Modules:
  0.0 791.6 jit_solution(12172388770690643116)
XLA Ops:
  8.0 0.0 copy-start.4
  8.0 0.0 all-reduce.7.cloned.1.call-start
  8.1 1.7 fusion.61
  9.8 0.7 bitcast_convert_fusion
  10.5 1.7 fusion.59
  12.2 0.7 bitcast_convert_fusion.1
  13.0 31.3 %all_gather.12 = bf16[256,256]{1,0:T(8,128)(2,1)S(1)} all-gather(bf16[16,256]{1,0:T(8,128)(2,1)S(1)} %bitcast_convert_fusion), channel_id=1, replica_groups=mesh['row'=16,'col'=32] {'row'}, dimensions={0}, use_global_device_ids=true | all-gather | bytes 139264 | tf_op jit(solution)/shard_map/all_gather | solution.py:53
  44.3 0.0 copy-done.4
  44.3 65.9 %all_gather.13 = bf16[512,256]{1,0:T(8,128)(2,1)S(1)} all-gather(bf16[16,256]{1,0:T(8,128)(2,1)S(1)} %bitcast_convert_fusion.1), channel_id=1, replica_groups=mesh['row'=16,'col'=32] {'col'}, dimensions={0}, use_global_device_ids=true | all-gather | bytes 270336 | tf_op jit(solution)/shard_map/all_gather | solution.py:52
  110.3 0.0 copy-done.16
  110.4 6.1 while.28
  111.0 0.6 fusion.93
  113.5 0.0 copy-start.13
  113.6 1.7 multiply_reduce_fusion.10
  115.2 0.0 copy-done.13
  115.2 0.5 multiply_reduce_fusion.11
  115.7 0.1 add_dynamic-update-slice_fusion.10
  116.4 0.0 copy-start.1
  116.4 0.0 copy-start.3
  116.5 1.0 copy.16
  117.5 0.0 all-reduce.7.cloned.1.call-update
  117.5 0.0 copy-done.1
  117.5 0.0 copy-done.3
  117.5 0.0 copy-start.12
  117.5 0.0 reduce-scatter.7.cloned.1.call-start
  117.6 0.5 reduce-scatter.7.cloned.1.call-update
  118.1 0.0 reduce-scatter.5.cloned.1.call-start
  118.2 0.5 reduce-scatter.5.cloned.1.call-update
  118.7 0.0 all-reduce.5.cloned.1.call-start
  118.8 0.2 copy.17
  119.0 0.7 fusion.67
  119.6 275.4 %all-reduce.7.cloned.1.call-done = (f32[256,256]{1,0:T(8,128)}, f32[256,256]{1,0:T(8,128)}, f32[512,256]{0,1:T(8,128)}) async-done(((f32[256,256]{1,0:T(8,128)}, f32[256,256]{1,0:T(8,128)}, f32[512,256]{0,1:T(8,128)}), (f32[256,256]{1,0:T(8,128)}, f32[256,256]{1,0:T(8,128)}, f32[512,256]{0,1:T(8,128)})) %all-reduce.7.cloned.1.call-update) | async-done | bytes 1048592 | tf_op jit(solution)/shard_map/psum | solution.py:56
  395.1 1.5 abs_reduce_fusion.3
  396.6 0.0 copy-start.10
  396.6 1.7 fusion.69
  398.4 0.0 copy-start.11
  398.4 0.1 copy.21
  398.6 0.0 reduce-scatter.7.cloned.1.call-done
  398.6 1.6 fusion.68
  400.2 29.4 %all_gather.14 = bf16[256,256]{1,0:T(8,128)(2,1)S(1)} all-gather(bf16[16,256]{1,0:T(8,128)(2,1)S(1)} %get-tuple-element.215), channel_id=1, replica_groups=mesh['row'=16,'col'=32] {'row'}, dimensions={0}, use_global_device_ids=true | all-gather | bytes 139264 | tf_op jit(solution)/shard_map/all_gather | solution.py:53
  429.6 0.9 fusion.71
  430.5 1.6 fusion.70
  432.1 56.0 %all_gather.15 = bf16[512,256]{1,0:T(8,128)(2,1)S(1)} all-gather(bf16[16,256]{1,0:T(8,128)(2,1)S(1)} %get-tuple-element.219), channel_id=1, replica_groups=mesh['row'=16,'col'=32] {'col'}, dimensions={0}, use_global_device_ids=true | all-gather | bytes 270336 | tf_op jit(solution)/shard_map/all_gather | solution.py:52
  488.1 1.0 fusion.72
  489.2 6.2 while.29
  489.9 0.7 fusion.96
  492.5 0.0 copy-start.14
  492.5 1.7 multiply_reduce_fusion.12
  494.2 0.5 multiply_reduce_fusion.13
  494.7 0.1 add_dynamic-update-slice_fusion.12
  495.4 1.0 copy.23
  496.4 0.0 all-reduce.5.cloned.1.call-update
  496.5 0.0 copy-done
  496.5 0.0 copy-done.2
  496.5 0.0 reduce-scatter.11.cloned.1.call-start
  496.5 0.5 reduce-scatter.11.cloned.1.call-update
  497.1 0.0 reduce-scatter.9.cloned.1.call-start
  497.1 0.7 reduce-scatter.9.cloned.1.call-update
  497.8 277.9 %all-reduce.5.cloned.1.call-done = (f32[256,256]{1,0:T(8,128)}, f32[256,256]{1,0:T(8,128)}, f32[512,256]{0,1:T(8,128)}) async-done(((f32[256,256]{1,0:T(8,128)}, f32[256,256]{1,0:T(8,128)}, f32[512,256]{0,1:T(8,128)}), (f32[256,256]{1,0:T(8,128)}, f32[256,256]{1,0:T(8,128)}, f32[512,256]{0,1:T(8,128)})) %all-reduce.5.cloned.1.call-update) | async-done | bytes 1048592 | tf_op jit(solution)/shard_map/psum | solution.py:56
  775.7 1.5 abs_reduce_fusion
  777.3 1.4 fusion.30
  778.7 1.0 copy.25
  779.7 2.2 fusion.35
  781.9 2.1 fusion.40
  (42 shorter events, 0.4 us)
Async XLA Ops:
  8.0 36.3 %copy-start.4 = (f32[512,256]{1,0:T(8,128)S(1)}, f32[512,256]{1,0:T(8,128)}, u32[]{:S(2)}) copy-start(f32[512,256]{1,0:T(8,128)} %param.17) | copy-start | bytes 1572868
  8.0 387.1 %all-reduce.7.cloned.1.call-start = ((), (), s32[]{:S(2)}) async-start(), calls=%async_computation.9 | async-start | bytes 2097152 | tf_op jit(solution)/shard_map/psum | solution.py:56
  44.3 66.1 %copy-start.16 = (s32[1,1,3,2]{2,3,1,0:T(2,128)S(1)}, s32[1,1,3,2]{2,3,1,0:T(2,128)}, u32[]{:S(2)}) copy-start(s32[1,1,3,2]{2,3,1,0:T(2,128)} %param.12) | copy-start | bytes 76
  113.5 1.7 copy-start.13
  116.4 1.1 copy-start.1
  116.4 1.1 copy-start.3
  117.5 1.4 copy-start.12
  117.5 281.0 %reduce-scatter.7.cloned.1.call-start = ((), (), s32[]{:S(2)}) async-start(), calls=%async_computation.5 | async-start | bytes 278528 | tf_op jit(solution)/shard_map/reduce_scatter | solution.py:83
  118.1 312.4 %reduce-scatter.5.cloned.1.call-start = ((), (), s32[]{:S(2)}) async-start(), calls=%async_computation.4 | async-start | bytes 540672 | tf_op jit(solution)/shard_map/reduce_scatter | solution.py:82
  118.7 657.0 %all-reduce.5.cloned.1.call-start = ((), (), s32[]{:S(2)}) async-start(), calls=%async_computation.8 | async-start | bytes 2097152 | tf_op jit(solution)/shard_map/psum | solution.py:56
  395.1 1.5 copy-start.5
  395.1 1.5 copy-start.6
  395.1 1.5 copy-start.9
  396.6 2.0 copy-start.10
  398.4 32.1 %copy-start.11 = (f32[1,16,256]{2,1,0:T(8,128)S(1)}, f32[1,16,256]{2,1,0:T(8,128)}, u32[]{:S(2)}) copy-start(f32[1,16,256]{2,1,0:T(8,128)} %param.15) | copy-start | bytes 49156
  492.5 1.7 copy-start.14
  495.4 1.1 copy-start
  495.4 1.1 copy-start.2
  496.5 283.2 %reduce-scatter.11.cloned.1.call-start = ((), (), s32[]{:S(2)}) async-start(), calls=%async_computation.7 | async-start | bytes 278528 | tf_op jit(solution)/shard_map/reduce_scatter | solution.py:83
  497.1 284.8 %reduce-scatter.9.cloned.1.call-start = ((), (), s32[]{:S(2)}) async-start(), calls=%async_computation.6 | async-start | bytes 540672 | tf_op jit(solution)/shard_map/reduce_scatter | solution.py:82
  775.7 1.5 copy-start.7
  775.7 1.5 copy-start.8
  775.7 1.5 copy-start.15
Sparse Core Ops, SparseCore 0:
  117.6 277.4 all-reduce.6
  496.6 279.0 all-reduce.4
Sparse Core Ops, SparseCore 1:
  120.8 68.2 reduce-scatter.6
  193.5 133.6 reduce-scatter.4
  499.8 69.9 reduce-scatter.10
  574.3 133.7 reduce-scatter.8
where the time goes:
time: 793 us; the launch traced here: 792 us
  waiting for transfers between devices  556 us (70%)
  blocking collectives  183 us (23%)
  matrix products  23.2 us (3%)
  between operations  16 us (2%)
    psum x2, waiting for transfers between devices, shards(): gram_a, gram_b = lax.psum((local_ga, local_gb), ('row', 'col'))  553 us
    all_gather x2, blocking collectives, shards(): a_range = lax.all_gather(a_bf, 'col', axis=0, tiled=True)  122 us
    all_gather x2, blocking collectives, shards(): b_range = lax.all_gather(b_bf, 'row', axis=0, tiled=True)  60.7 us
  transfers between devices with their start and end apart: 6, of which 2 were waited for; matrix products, arithmetic and copies ran while one was open for 2% of the time, Pallas kernels for 0%

commit v1 on v0

--- a/solution.py
+++ b/solution.py
@@ -53,7 +53,7 @@
         b_range = lax.all_gather(b_bf, "row", axis=0, tiled=True)
         local_ga = gram(a_bf)
         local_gb = gram(b_bf)
-        gram_a, gram_b = lax.psum((local_ga, local_gb), ("row", "col"))
+        gram_a, gram_b = jax.lax.psum(jax.lax.psum((local_ga, local_gb), "row"), "col")
         gram_c = gram(c_bf)
 
         def own_step(slot, carry):

time: 793 us -> 2030 us (2.56)
  the two profiles are of different devices: /device:TPU:17 before, /device:TPU:64 now
where the time goes in v1:
time: 2030 us
  waiting for transfers between devices  1790 us (88%)
  blocking collectives  186 us (9%)
  matrix products  25.2 us (1%)
    psum x2, waiting for transfers between devices, shards(): jax.lax.psum(jax.lax.psum((local_ga, local_gb), 'row'), 'col')  660 us
    psum x2, waiting for transfers between devices, shards(): summed_c = lax.psum(drive_c, ('row', 'col'))  551 us
    reduce_scatter x2, waiting for transfers between devices, shards(): mine_a = lax.psum_scatter(drive_a, 'col', scatter_dimension=0, tiled=True)  259 us
    reduce_scatter x2, waiting for transfers between devices, shards(): mine_b = lax.psum_scatter(drive_b, 'row', scatter_dimension=0, tiled=True)  167 us
    psum x2, waiting for transfers between devices, shards(): jax.lax.psum((local_ga, local_gb), 'row')  152 us
    all_gather x2, blocking collectives, shards(): a_range = lax.all_gather(a_bf, 'col', axis=0, tiled=True)  100 us
    all_gather x2, blocking collectives, shards(): b_range = lax.all_gather(b_bf, 'row', axis=0, tiled=True)  86.1 us
  transfers between devices with their start and end apart: 10, of which 10 were waited for; matrix products, arithmetic and copies ran while one was open for 1% of the time, Pallas kernels for 0%

profile of v1, /device:TPU:64, one launch (start us, length us, event | category | flops | bytes accessed | tf_op | source)
XLA Modules:
  0.0 2032.3 jit_solution(9842912187677325405)
XLA Ops:
  7.2 0.0 all-reduce.21.cloned.1.call-start
  7.2 1.7 fusion.61
  9.0 1.7 fusion.59
  10.7 0.0 all-reduce.21.cloned.1.call-update
  10.7 0.0 all-reduce.17.cloned.1.call-start
  10.8 44.0 %all_gather.12 = bf16[256,256]{1,0:T(8,128)(2,1)S(1)} all-gather(bf16[16,256]{1,0:T(8,128)(2,1)S(1)} %bitcast_convert_fusion), channel_id=1, replica_groups=mesh['row'=16,'col'=32] {'row'}, dimensions={0}, use_global_device_ids=true | all-gather | bytes 139264 | tf_op jit(solution)/shard_map/all_gather | solution.py:53
  54.9 50.3 %all_gather.13 = bf16[512,256]{1,0:T(8,128)(2,1)S(1)} all-gather(bf16[16,256]{1,0:T(8,128)(2,1)S(1)} %bitcast_convert_fusion.1), channel_id=1, replica_groups=mesh['row'=16,'col'=32] {'col'}, dimensions={0}, use_global_device_ids=true | all-gather | bytes 270336 | tf_op jit(solution)/shard_map/all_gather | solution.py:52
  105.1 78.4 %all-reduce.21.cloned.1.call-done = (f32[256,256]{1,0:T(8,128)}, f32[256,256]{1,0:T(8,128)}) async-done(((f32[256,256]{1,0:T(8,128)}, f32[256,256]{1,0:T(8,128)}), (f32[256,256]{1,0:T(8,128)}, f32[256,256]{1,0:T(8,128)})) %all-reduce.21.cloned.1.call-update) | async-done | bytes 524304 | tf_op jit(solution)/shard_map/psum | solution.py:56
  183.6 0.0 all-reduce.17.cloned.1.call-update
  183.6 0.0 reduce-scatter.5.cloned.1.call-start
  183.8 6.2 while.28
  184.5 0.7 fusion.93
  187.1 1.7 multiply_reduce_fusion.10
  188.8 0.4 multiply_reduce_fusion.11
  189.3 0.1 add_dynamic-update-slice_fusion.10
  190.0 0.8 copy-done.1
  190.8 0.0 reduce-scatter.5.cloned.1.call-update
  190.8 0.0 reduce-scatter.7.cloned.1.call-start
  190.9 0.0 copy-done.3
  190.9 0.5 reduce-scatter.7.cloned.1.call-update
  191.4 0.0 all-reduce.11.cloned.1.call-start
  191.4 1.0 copy.16
  192.4 0.0 all-reduce.11.cloned.1.call-update
  192.5 0.0 all-reduce.19.cloned.1.call-start
  192.5 0.2 copy.17
  192.7 0.4 copy-done.11
  193.1 0.6 fusion.67
  193.7 329.4 %all-reduce.17.cloned.1.call-done = (f32[256,256]{1,0:T(8,128)}, f32[256,256]{1,0:T(8,128)}) async-done(((f32[256,256]{1,0:T(8,128)}, f32[256,256]{1,0:T(8,128)}), (f32[256,256]{1,0:T(8,128)}, f32[256,256]{1,0:T(8,128)})) %all-reduce.17.cloned.1.call-update) | async-done | bytes 524304 | tf_op jit(solution)/shard_map/psum | solution.py:56
  523.1 1.5 abs_reduce_fusion.3
  524.6 135.3 %reduce-scatter.5.cloned.1.call-done = f32[16,256]{1,0:T(8,128)} async-done(((f32[512,256]{1,0:T(8,128)}), f32[16,256]{1,0:T(8,128)}) %reduce-scatter.5.cloned.1.call-update) | async-done | bytes 16400 | tf_op jit(solution)/shard_map/reduce_scatter | solution.py:82
  659.9 1.7 fusion.70
  661.6 83.9 %reduce-scatter.7.cloned.1.call-done = f32[16,256]{1,0:T(8,128)} async-done(((f32[256,256]{1,0:T(8,128)}), f32[16,256]{1,0:T(8,128)}) %reduce-scatter.7.cloned.1.call-update) | async-done | bytes 16400 | tf_op jit(solution)/shard_map/reduce_scatter | solution.py:83
  745.5 1.6 fusion.68
  747.2 0.9 fusion.71
  748.1 0.9 fusion.72
  749.0 0.0 all-reduce.19.cloned.1.call-update
  749.0 0.0 all-reduce.15.cloned.1.call-start
  749.1 269.6 %all-reduce.11.cloned.1.call-done = f32[512,256]{0,1:T(8,128)} async-done(((f32[512,256]{0,1:T(8,128)}), f32[512,256]{0,1:T(8,128)}) %all-reduce.11.cloned.1.call-update) | async-done | bytes 524304 | tf_op jit(solution)/shard_map/psum | solution.py:84
  1018.7 2.8 fusion.69
  1021.5 0.1 copy.21
  1021.6 42.1 %all_gather.14 = bf16[256,256]{1,0:T(8,128)(2,1)S(1)} all-gather(bf16[16,256]{1,0:T(8,128)(2,1)S(1)} %get-tuple-element.217), channel_id=1, replica_groups=mesh['row'=16,'col'=32] {'row'}, dimensions={0}, use_global_device_ids=true | all-gather | bytes 139264 | tf_op jit(solution)/shard_map/all_gather | solution.py:53
  1063.7 50.0 %all_gather.15 = bf16[512,256]{1,0:T(8,128)(2,1)S(1)} all-gather(bf16[16,256]{1,0:T(8,128)(2,1)S(1)} %get-tuple-element.221), channel_id=1, replica_groups=mesh['row'=16,'col'=32] {'col'}, dimensions={0}, use_global_device_ids=true | all-gather | bytes 270336 | tf_op jit(solution)/shard_map/all_gather | solution.py:52
  1113.7 73.6 %all-reduce.19.cloned.1.call-done = (f32[256,256]{1,0:T(8,128)}, f32[256,256]{1,0:T(8,128)}) async-done(((f32[256,256]{1,0:T(8,128)}, f32[256,256]{1,0:T(8,128)}), (f32[256,256]{1,0:T(8,128)}, f32[256,256]{1,0:T(8,128)})) %all-reduce.19.cloned.1.call-update) | async-done | bytes 524304 | tf_op jit(solution)/shard_map/psum | solution.py:56
  1187.3 0.0 all-reduce.13.cloned.1.call-start
  1187.4 6.1 while.29
  1188.1 0.6 fusion.96
  1190.6 1.7 multiply_reduce_fusion.12
  1192.3 0.5 multiply_reduce_fusion.13
  1192.8 0.1 add_dynamic-update-slice_fusion.12
  1193.5 1.0 copy.23
  1194.6 0.0 all-reduce.13.cloned.1.call-update
  1194.6 0.0 reduce-scatter.9.cloned.1.call-start
  1194.6 0.7 reduce-scatter.9.cloned.1.call-update
  1195.3 0.0 reduce-scatter.11.cloned.1.call-start
  1195.4 0.5 reduce-scatter.11.cloned.1.call-update
  1195.9 330.9 %all-reduce.15.cloned.1.call-done = (f32[256,256]{1,0:T(8,128)}, f32[256,256]{1,0:T(8,128)}) async-done(((f32[256,256]{1,0:T(8,128)}, f32[256,256]{1,0:T(8,128)}), (f32[256,256]{1,0:T(8,128)}, f32[256,256]{1,0:T(8,128)})) %all-reduce.15.cloned.1.call-update) | async-done | bytes 524304 | tf_op jit(solution)/shard_map/psum | solution.py:56
  1526.8 1.5 abs_reduce_fusion
  1528.3 281.8 %all-reduce.13.cloned.1.call-done = f32[512,256]{0,1:T(8,128)} async-done(((f32[512,256]{0,1:T(8,128)}), f32[512,256]{0,1:T(8,128)}) %all-reduce.13.cloned.1.call-update) | async-done | bytes 524304 | tf_op jit(solution)/shard_map/psum | solution.py:84
  1810.1 2.4 fusion.30
  1812.5 1.0 copy.25
  1813.5 124.1 %reduce-scatter.9.cloned.1.call-done = f32[16,256]{1,0:T(8,128)} async-done(((f32[512,256]{1,0:T(8,128)}), f32[16,256]{1,0:T(8,128)}) %reduce-scatter.9.cloned.1.call-update) | async-done | bytes 16400 | tf_op jit(solution)/shard_map/reduce_scatter | solution.py:82
  1937.6 2.2 fusion.40
  1939.8 83.5 %reduce-scatter.11.cloned.1.call-done = f32[16,256]{1,0:T(8,128)} async-done(((f32[256,256]{1,0:T(8,128)}), f32[16,256]{1,0:T(8,128)}) %reduce-scatter.11.cloned.1.call-update) | async-done | bytes 16400 | tf_op jit(solution)/shard_map/reduce_scatter | solution.py:83
  2023.3 2.1 fusion.35
  (50 shorter events, 0.4 us)
Async XLA Ops:
  7.2 3.6 copy-start.10
  7.2 47.7 %copy-start.9 = (f32[1,16,256]{2,1,0:T(8,128)S(1)}, f32[1,16,256]{2,1,0:T(8,128)}, u32[]{:S(2)}) copy-start(f32[1,16,256]{2,1,0:T(8,128)} %param.15) | copy-start | bytes 49156
  7.2 3.6 copy-start.4
  7.2 176.4 %all-reduce.21.cloned.1.call-start = ((), (), s32[]{:S(2)}) async-start(), calls=%async_computation.13 | async-start | bytes 1048576 | tf_op jit(solution)/shard_map/psum | solution.py:56
  10.7 512.4 %all-reduce.17.cloned.1.call-start = ((), (), s32[]{:S(2)}) async-start(), calls=%async_computation.11 | async-start | bytes 1048576 | tf_op jit(solution)/shard_map/psum | solution.py:56
  54.9 128.9 %copy-start.14 = (s32[1,1,3,2]{2,3,1,0:T(2,128)S(1)}, s32[1,1,3,2]{2,3,1,0:T(2,128)}, u32[]{:S(2)}) copy-start(s32[1,1,3,2]{2,3,1,0:T(2,128)} %param.12) | copy-start | bytes 76
  183.6 476.3 %reduce-scatter.5.cloned.1.call-start = ((), (), s32[]{:S(2)}) async-start(), calls=%async_computation.4 | async-start | bytes 540672 | tf_op jit(solution)/shard_map/reduce_scatter | solution.py:82
  187.1 1.7 copy-start.12
  190.0 0.8 copy-start.1
  190.0 0.9 copy-start.3
  190.8 554.7 %reduce-scatter.7.cloned.1.call-start = ((), (), s32[]{:S(2)}) async-start(), calls=%async_computation.5 | async-start | bytes 278528 | tf_op jit(solution)/shard_map/reduce_scatter | solution.py:83
  191.4 827.3 %all-reduce.11.cloned.1.call-start = ((), (), s32[]{:S(2)}) async-start(), calls=%async_computation.6 | async-start | bytes 1048576 | tf_op jit(solution)/shard_map/psum | solution.py:84
  192.4 0.7 copy-start.11
  192.5 994.8 %all-reduce.19.cloned.1.call-start = ((), (), s32[]{:S(2)}) async-start(), calls=%async_computation.12 | async-start | bytes 1048576 | tf_op jit(solution)/shard_map/psum | solution.py:56
  523.1 136.8 %copy-start.5 = (f32[256,256]{1,0:T(8,128)S(1)}, f32[256,256]{1,0:T(8,128)}, u32[]{:S(2)}) copy-start(f32[256,256]{1,0:T(8,128)} %get-tuple-element.194) | copy-start | bytes 786436
  523.1 222.4 %copy-start.6 = (f32[256,256]{1,0:T(8,128)S(1)}, f32[256,256]{1,0:T(8,128)}, u32[]{:S(2)}) copy-start(f32[256,256]{1,0:T(8,128)} %get-tuple-element.195) | copy-start | bytes 786436
  749.0 777.8 %all-reduce.15.cloned.1.call-start = ((), (), s32[]{:S(2)}) async-start(), calls=%async_computation.10 | async-start | bytes 1048576 | tf_op jit(solution)/shard_map/psum | solution.py:56
  1187.3 622.8 %all-reduce.13.cloned.1.call-start = ((), (), s32[]{:S(2)}) async-start(), calls=%async_computation.9 | async-start | bytes 1048576 | tf_op jit(solution)/shard_map/psum | solution.py:84
  1190.6 1.7 copy-start.13
  1193.5 1.1 copy-start
  1193.5 1.8 copy-start.2
  1194.6 743.1 %reduce-scatter.9.cloned.1.call-start = ((), (), s32[]{:S(2)}) async-start(), calls=%async_computation.7 | async-start | bytes 540672 | tf_op jit(solution)/shard_map/reduce_scatter | solution.py:82
  1195.3 828.0 %reduce-scatter.11.cloned.1.call-start = ((), (), s32[]{:S(2)}) async-start(), calls=%async_computation.8 | async-start | bytes 278528 | tf_op jit(solution)/shard_map/reduce_scatter | solution.py:83
  1526.8 283.3 %copy-start.7 = (f32[256,256]{1,0:T(8,128)S(1)}, f32[256,256]{1,0:T(8,128)}, u32[]{:S(2)}) copy-start(f32[256,256]{1,0:T(8,128)} %get-tuple-element.193) | copy-start | bytes 786436
  1526.8 283.3 %copy-start.8 = (f32[256,256]{1,0:T(8,128)S(1)}, f32[256,256]{1,0:T(8,128)}, u32[]{:S(2)}) copy-start(f32[256,256]{1,0:T(8,128)} %get-tuple-element.192) | copy-start | bytes 786436
Sparse Core Ops, SparseCore 0:
  11.5 172.0 all-reduce.20
  186.5 336.5 all-reduce.16
  528.3 131.5 reduce-scatter.4
  662.6 82.9 reduce-scatter.6
  750.4 268.2 all-reduce.10
  1022.1 165.1 all-reduce.18
  1190.2 336.5 all-reduce.14
  1532.4 277.6 all-reduce.12
  1814.7 122.8 reduce-scatter.8
  1940.3 82.9 reduce-scatter.10
